TPU v7x, 32 devices: a whole 2x2x4 slice. The times are simulated.
32 devices in a mesh: heads: 2 (over x), ctx: 16 (over z, y, core).
Axes of the slice: x: 2, y: 2, z: 4, core: 2. Of those that a mesh axis runs over, the one named last changes fastest.
Arguments:
- queries: bfloat16 [4096, 4096], P('ctx', 'heads'), may hold values from -80 to 80
- keys: bfloat16 [4096, 1024], P('ctx', 'heads'), may hold values from -4.5 to 4.5
- values: bfloat16 [4096, 1024], P('ctx', 'heads'), may hold values from -6 to 6
- doc_ids: int32 [4096], P('ctx'), may hold values from 0 to 3, never falling along the last dimension, each value on 1 to 2048 neighbouring positions
- out_weight: bfloat16 [4096, 4096], P('heads', 'ctx'), may hold values from -0.09375 to 0.09375
Outputs:
- mixed: bfloat16 [4096, 4096], P('ctx', 'heads')
Inputs may be any that keep to these rules, and one draw needn't show every extreme that they name: `doc_ids`: document ids never fall along the tokens; each document has at most 2048 tokens.
All inputs are finite; a program needn't handle non-finite values.
Results may differ from a plain program's by a relative error of at most 0.015.
Values may be sent and summed in bfloat16 or wider, within the bound.
A program may use at most 64 MiB of HBM per device.

v0:
```python
import functools
import math

import jax
import jax.numpy as jnp
from jax import lax
from jax.experimental import pallas as pl
from jax.experimental.pallas import tpu as pltpu
from jax.sharding import PartitionSpec as P

HEAD_SIZE = 128
LOOKBACK_WINDOW = 4096
QPG = 4


PLANE = 4
DOC_ROWS = 16
MESH = pl.DeviceIdType.MESH


def fused_kernel(
    planes, n_heads, groups, tok, wcols,
    q_ref, kv_hbm, w_hbm, out_ref,
    kvbuf, wbuf, abuf, acc, rowmax, total, bias, xsend, xrecv, keep, rsend, obuf,
    local_sem, kv_recv, kvz_send, kvp_send, kvf_send,
    w_recv, w_right, w_left, a_recv, a_send, a_fwd,
    x_send, x_recv, o_send, o_recv,
):
    h = lax.axis_index("heads")
    c = lax.axis_index("ctx")
    z = c // PLANE
    p = c % PLANE
    core = p % 2
    row = p // 2
    mate = p + 1 - 2 * core
    across = (p + 2) % PLANE
    diag = (mate + 2) % PLANE
    last = planes - 1
    kdim = groups * HEAD_SIZE
    span = QPG * groups
    per_half = planes // n_heads
    half = wcols // 2

    def in_plane(other):
        return (h, z * PLANE + other)

    up = (h, c + PLANE)
    down = (h, c - PLANE)

    def copy(src, dst, send, recv, dev):
        return pltpu.make_async_remote_copy(
            src_ref=src, dst_ref=dst, send_sem=send, recv_sem=recv,
            device_id=dev, device_id_type=MESH,
        )

    def kv_up(d):
        return copy(kvbuf.at[d, p], kvbuf.at[d + 1, p], kvz_send.at[d], kv_recv.at[d + 1, p], up)

    def kv_side(d, which):
        dev = in_plane(mate if which == 0 else across)
        return copy(kvbuf.at[d, p], kvbuf.at[d, p], kvp_send.at[d, which], kv_recv.at[d, p], dev)

    def kv_forward(d):
        return copy(
            kvbuf.at[d, across], kvbuf.at[d, across], kvf_send.at[d], kv_recv.at[d, across],
            in_plane(mate),
        )

    def kv_wait(d, who):
        copy(
            kvbuf.at[d, who], kvbuf.at[d, who], kvf_send.at[d], kv_recv.at[d, who], in_plane(mate)
        ).wait_recv()

    def w_up(j, s):
        ref = wbuf.at[j, s]
        return copy(ref, ref, w_right.at[j, s], w_recv.at[j, s], up)

    def w_down(j, s):
        ref = wbuf.at[j, s]
        return copy(ref, ref, w_left.at[j, s], w_recv.at[j, s], down)

    def w_wait(j, s):
        ref = wbuf.at[j, s]
        copy(ref, ref, w_left.at[j, s], w_recv.at[j, s], in_plane(mate)).wait_recv()

    def w_from_above(j):
        for s in range(2):
            w_wait(j, s)

            @pl.when(z > 0)
            def _():
                w_down(j, s).start()

    def w_from_below(j):
        for s in range(2):
            w_wait(j, s)

            @pl.when(z < last)
            def _():
                w_up(j, s).start()

    def target(k):
        return jnp.where(k == 0, across, jnp.where(k == 1, diag, jnp.where(k == 2, mate, p)))

    def a_side(which):
        dev = in_plane(mate if which == 0 else across)
        return copy(abuf.at[p], abuf.at[p], a_send.at[which], a_recv.at[p], dev)

    def a_forward():
        return copy(abuf.at[across], abuf.at[across], a_fwd, a_recv.at[across], in_plane(mate))

    def a_wait(who):
        copy(abuf.at[who], abuf.at[who], a_fwd, a_recv.at[who], in_plane(mate)).wait_recv()

    def x_copy(u, pp):
        return copy(
            xsend.at[u, pp], xrecv.at[u, pp], x_send.at[u, pp], x_recv.at[u, pp], (1 - h, c)
        )

    def o_copy(u, pp):
        return copy(
            rsend.at[u, pp], obuf.at[u, p], o_send.at[u, pp], o_recv.at[u, p], in_plane(pp)
        )

    kv_in = pltpu.make_async_copy(kv_hbm, kvbuf.at[0, p], local_sem.at[0])
    w_in = [
        pltpu.make_async_copy(
            w_hbm.at[:, s * half : (s + 1) * half], wbuf.at[z, s], local_sem.at[1 + s]
        )
        for s in range(2)
    ]
    kv_in.start()
    w_in[0].start()
    w_in[1].start()

    barrier = pltpu.get_barrier_semaphore()
    for dev in (in_plane(mate), in_plane(across), in_plane(diag), (1 - h, c)):
        pl.semaphore_signal(barrier, inc=1, device_id=dev, device_id_type=MESH)

    @pl.when(z < last)
    def _():
        pl.semaphore_signal(barrier, inc=1, device_id=up, device_id_type=MESH)

    @pl.when(z > 0)
    def _():
        pl.semaphore_signal(barrier, inc=1, device_id=down, device_id_type=MESH)

    pl.semaphore_wait(barrier, 4 + jnp.minimum(z, 1) + jnp.minimum(last - z, 1))

    kv_in.wait()

    @pl.when(z < last)
    def _():
        kv_up(0).start()

    @pl.when(row == 0)
    def _():
        kv_side(0, 1).start()

    @pl.when(core == 0)
    def _():
        kv_side(0, 0).start()

    w_in[0].wait()
    w_in[1].wait()

    @pl.when(z > 0)
    def _():
        w_down(z, 0).start()
        w_down(z, 1).start()

    factor = HEAD_SIZE ** (-0.5) * math.log2(math.e)

    def docs_of(block):
        return block[tok : tok + DOC_ROWS, 0:tok].astype(jnp.float32)[0:1, :]

    def attend(d, who, first):
        block = kvbuf.at[d, who]
        kdoc = jnp.broadcast_to(docs_of(block), (tok, tok)).T
        vis = kdoc == docs_of(kvbuf.at[0, p])
        if first:
            kpos = lax.broadcasted_iota(jnp.int32, (tok, tok), 0)
            qpos = lax.broadcasted_iota(jnp.int32, (tok, tok), 1)
            vis = vis & (kpos <= qpos)
        bias[...] = jnp.where(vis, jnp.float32(0.0), jnp.float32(-1e30))

        def group(g, carry):
            keys = block[0:tok, pl.ds(pl.multiple_of(g * HEAD_SIZE, HEAD_SIZE), HEAD_SIZE)]
            vals = block[0:tok, pl.ds(pl.multiple_of(kdim + g * HEAD_SIZE, HEAD_SIZE), HEAD_SIZE)]
            for n in range(QPG):
                head = g * QPG + n
                qs = q_ref[:, pl.ds(pl.multiple_of(head * HEAD_SIZE, HEAD_SIZE), HEAD_SIZE)]
                scores = lax.dot_general(
                    keys, qs, (((1,), (1,)), ((), ())), preferred_element_type=jnp.float32
                ) + bias[...]
                top = jnp.max(scores, axis=0, keepdims=True)
                if not first:
                    old = rowmax[head]
                    top = jnp.maximum(old, top)
                weights = jnp.exp2((scores - top) * factor)
                sums = jnp.sum(weights, axis=0, keepdims=True)
                contrib = lax.dot_general(
                    vals, weights.astype(jnp.bfloat16), (((0,), (0,)), ((), ())),
                    preferred_element_type=jnp.float32,
                )
                if first:
                    total[head] = sums
                    acc[head] = contrib
                else:
                    shrink = jnp.exp2((old - top) * factor)
                    total[head] = total[head] * shrink + sums
                    acc[head] = acc[head] * shrink + contrib
                rowmax[head] = top
            return carry

        lax.fori_loop(0, groups, group, 0)

    attend(0, p, True)

    @pl.when(z > 0)
    def _():
        kv_wait(1, p)

        @pl.when(z < last)
        def _():
            kv_up(1).start()

        kv_side(1, 1).start()
        kv_side(1, 0).start()

    @pl.when(z < last)
    def _():
        w_up(z, 0).start()
        w_up(z, 1).start()

    @pl.when(row == 1)
    def _():
        kv_wait(0, across)
        kv_forward(0).start()

    @pl.when(core == 1)
    def _():
        kv_wait(0, mate)

    @pl.when(row == 1)
    def _():
        kv_wait(0, diag)

    def block_loop(d, lo, hi):
        def one(who, carry):
            attend(d, who, False)
            return carry

        lax.fori_loop(lo, hi, one, 0)

    block_loop(0, 0, p)

    @pl.when(z > 0)
    def _():
        kv_wait(1, across)
        kv_forward(1).start()

    @pl.when(z > 1)
    def _():
        kv_wait(2, p)

        @pl.when(row == 1)
        def _():
            kv_side(2, 1).start()

        @pl.when(core == 1)
        def _():
            kv_side(2, 0).start()

    @pl.when(z < last)
    def _():
        w_from_above(z + 1)

    @pl.when(z > 0)
    def _():
        kv_wait(1, mate)
        kv_wait(1, diag)
        block_loop(1, 0, PLANE)

    @pl.when((z > 0) & (z < last))
    def _():
        w_from_below(z - 1)

    @pl.when((z > 0) & (z + 2 < planes))
    def _():
        w_from_above(z + 2)

    @pl.when(z > 1)
    def _():
        @pl.when(row == 0)
        def _():
            kv_wait(2, across)
            kv_forward(2).start()

        @pl.when(core == 0)
        def _():
            kv_wait(2, mate)

        @pl.when(row == 0)
        def _():
            kv_wait(2, diag)

        block_loop(2, p, PLANE)

    def finish_head(head, carry):
        cols = pl.ds(pl.multiple_of(head * HEAD_SIZE, HEAD_SIZE), HEAD_SIZE)
        abuf[p, :, cols] = (acc[head] / total[head]).T.astype(jnp.bfloat16)
        return carry

    lax.fori_loop(0, span, finish_head, 0)
    a_side(1).start()
    a_side(0).start()

    @pl.when(z == last)
    def _():
        w_from_below(z - 1)

    @pl.when((z == 0) & (z + 2 < planes))
    def _():
        w_from_above(z + 2)

    @pl.when(z > 1)
    def _():
        w_from_below(z - 2)

    def plane_of(i):
        dist = (i + 1) // 2
        return z + dist * (2 * (i % 2) - 1)

    def exists(j):
        return (j >= 0) & (j < planes)

    def place(u, pp, part):
        j = u // 2
        mine = (j // per_half) == h
        uu = u % (2 * per_half)

        @pl.when(mine)
        def _():
            keep[uu, pp] = part

        @pl.when(jnp.logical_not(mine))
        def _():
            xsend[uu, pp] = part.astype(jnp.bfloat16)
            x_copy(uu, pp).start()

    def project(i, lo, hi):
        j = plane_of(i)

        @pl.when(exists(j))
        def _():
            @pl.when(i >= 5)
            def _():
                w_wait(j, 0)
                w_wait(j, 1)

            def rows(k, carry):
                pp = target(k)
                both = jnp.concatenate([wbuf[j, 0], wbuf[j, 1]], axis=1)
                part = jnp.dot(abuf[pp], both, preferred_element_type=jnp.float32)
                place(2 * j, pp, part[:, :half])
                place(2 * j + 1, pp, part[:, half:])
                return carry

            lax.fori_loop(lo, hi, rows, 0)

    def project_half(i, s):
        j = plane_of(i)

        @pl.when(exists(j))
        def _():
            w_wait(j, s)

            def rows(k, carry):
                pp = target(k)
                part = jnp.dot(abuf[pp], wbuf[j, s], preferred_element_type=jnp.float32)
                place(2 * j + s, pp, part)
                return carry

            lax.fori_loop(0, PLANE, rows, 0)

    def finish(i, s):
        j = plane_of(i)

        @pl.when(exists(j) & ((j // per_half) == h))
        def _():
            u = (2 * j + s) % (2 * per_half)

            def rows(k, carry):
                pp = target(k)
                x_copy(u, pp).wait_recv()
                done = (keep[u, pp] + xrecv[u, pp].astype(jnp.float32)).astype(jnp.bfloat16)

                @pl.when(pp == p)
                def _():
                    out_ref[:, column(u, p)] = done

                @pl.when(pp != p)
                def _():
                    rsend[u, pp] = done
                    o_copy(u, pp).start()

                return carry

            lax.fori_loop(0, PLANE, rows, 0)

    def column(u, src):
        return pl.ds(pl.multiple_of(((u // 2) * PLANE + src) * wcols + (u % 2) * half, half), half)

    steps = 2 * planes - 1

    def near_step(i, carry):
        project(i, 2, PLANE)
        return carry

    def across_step(i, carry):
        project(i, 0, 2)
        return carry

    def finish_step(k, carry):
        finish(k // 2, k % 2)
        return carry

    a_wait(mate)
    lax.fori_loop(0, steps - 2, near_step, 0)
    a_wait(across)
    a_forward().start()
    a_wait(diag)
    lax.fori_loop(0, steps - 2, across_step, 0)
    project(steps - 2, 0, PLANE)
    def far_project(s, carry):
        project_half(steps - 1, s)
        return carry

    lax.fori_loop(0, 2, far_project, 0)
    lax.fori_loop(0, 2 * steps, finish_step, 0)

    def collect(k, carry):
        u = k // PLANE
        src = k % PLANE

        @pl.when(src != p)
        def _():
            copy(
                obuf.at[u, src], obuf.at[u, src], o_send.at[u, src], o_recv.at[u, src],
                in_plane(mate),
            ).wait_recv()
            out_ref[:, column(u, src)] = obuf[u, src]
            o_copy(u, src).wait_send()

        x_copy(u, src).wait_send()
        return carry

    lax.fori_loop(0, 2 * per_half * PLANE, collect, 0)

    a_side(0).wait_send()
    a_side(1).wait_send()
    a_forward().wait_send()

    def w_drain(j, carry):
        @pl.when((j <= z) & (z < last))
        def _():
            w_up(j, 0).wait_send()
            w_up(j, 1).wait_send()

        @pl.when((j >= z) & (z > 0))
        def _():
            w_down(j, 0).wait_send()
            w_down(j, 1).wait_send()

        return carry

    lax.fori_loop(0, planes, w_drain, 0)

    @pl.when(z < last)
    def _():
        kv_up(0).wait_send()

        @pl.when(z > 0)
        def _():
            kv_up(1).wait_send()

    @pl.when(row == 0)
    def _():
        kv_side(0, 1).wait_send()

    @pl.when(core == 0)
    def _():
        kv_side(0, 0).wait_send()

    @pl.when(row == 1)
    def _():
        kv_forward(0).wait_send()

    @pl.when(z > 0)
    def _():
        kv_side(1, 0).wait_send()
        kv_side(1, 1).wait_send()
        kv_forward(1).wait_send()

    @pl.when(z > 1)
    def _():
        @pl.when(row == 1)
        def _():
            kv_side(2, 1).wait_send()

        @pl.when(core == 1)
        def _():
            kv_side(2, 0).wait_send()

        @pl.when(row == 0)
        def _():
            kv_forward(2).wait_send()


def fused_body(n_ctx, n_heads, queries, keys, values, doc_ids, out_weight):
    tok, qcols = queries.shape
    kdim = keys.shape[1]
    groups = kdim // HEAD_SIZE
    krows, wcols = out_weight.shape
    planes = n_ctx // PLANE
    span = QPG * groups
    per_half = planes // n_heads
    width = 2 * kdim
    docs = jnp.broadcast_to(
        jnp.pad(doc_ids.astype(jnp.bfloat16), (0, width - tok))[None, :], (DOC_ROWS, width)
    )
    kv = jnp.concatenate([jnp.concatenate([keys, values], axis=1), docs], axis=0)
    bf, f32 = jnp.bfloat16, jnp.float32
    dma = pltpu.SemaphoreType.DMA
    return pl.pallas_call(
        functools.partial(fused_kernel, planes, n_heads, groups, tok, wcols),
        out_shape=jax.ShapeDtypeStruct((tok, per_half * PLANE * wcols), bf),
        in_specs=[
            pl.BlockSpec(memory_space=pltpu.VMEM),
            pl.BlockSpec(memory_space=pl.ANY),
            pl.BlockSpec(memory_space=pl.ANY),
        ],
        out_specs=pl.BlockSpec(memory_space=pltpu.VMEM),
        scratch_shapes=[
            pltpu.VMEM((3, PLANE, tok + DOC_ROWS, width), bf),
            pltpu.VMEM((planes, 2, krows, wcols // 2), bf),
            pltpu.VMEM((PLANE, tok, krows), bf),
            pltpu.VMEM((span, HEAD_SIZE, tok), f32),
            pltpu.VMEM((span, 1, tok), f32),
            pltpu.VMEM((span, 1, tok), f32),
            pltpu.VMEM((tok, tok), f32),
            pltpu.VMEM((2 * per_half, PLANE, tok, wcols // 2), bf),
            pltpu.VMEM((2 * per_half, PLANE, tok, wcols // 2), bf),
            pltpu.VMEM((2 * per_half, PLANE, tok, wcols // 2), f32),
            pltpu.VMEM((2 * per_half, PLANE, tok, wcols // 2), bf),
            pltpu.VMEM((2 * per_half, PLANE, tok, wcols // 2), bf),
            dma((3,)),
            dma((3, PLANE)),
            dma((2,)),
            dma((3, 2)),
            dma((3,)),
            dma((planes, 2)),
            dma((planes, 2)),
            dma((planes, 2)),
            dma((PLANE,)),
            dma((2,)),
            dma,
            dma((2 * per_half, PLANE)),
            dma((2 * per_half, PLANE)),
            dma((2 * per_half, PLANE)),
            dma((2 * per_half, PLANE)),
        ],
        compiler_params=pltpu.CompilerParams(
            collective_id=0, has_side_effects=True, vmem_limit_bytes=56 * 1024 * 1024
        ),
    )(queries, kv, out_weight)


def fits_fused(n_ctx, n_heads, queries, keys, out_weight):
    tokens = queries.shape[0]
    tok = tokens // n_ctx
    reach = min(LOOKBACK_WINDOW, tokens // 2)
    return (
        n_heads == 2
        and n_ctx % PLANE == 0
        and n_ctx // PLANE == 4
        and tok == 2 * HEAD_SIZE
        and reach == 2 * PLANE * tok
        and reach < LOOKBACK_WINDOW
        and 2 * keys.shape[1] // n_heads >= tok
        and (out_weight.shape[1] // n_ctx) % 256 == 0
        and keys.shape[1] // n_heads % HEAD_SIZE == 0
    )


def passed_along(block, axis, distance):
    devices = range(lax.axis_size(axis))
    route = [(i - distance, i) for i in devices if i - distance in devices]
    return lax.ppermute(block, axis, route)


def body(queries, keys, values, doc_ids, out_weight):
    tok_rows = queries.shape[0]
    groups = keys.shape[1] // HEAD_SIZE
    scale = HEAD_SIZE ** (-0.5)
    q_local = queries.reshape(tok_rows, groups, QPG, HEAD_SIZE)
    here = lax.axis_index("ctx")
    qpos = here * tok_rows + jnp.arange(tok_rows, dtype=jnp.int32)
    reach = LOOKBACK_WINDOW // tok_rows

    def work(state, kblk, vblk, sblk, kstart):
        rowmax, total, accum = state
        scores = (
            jnp.einsum(
                "tgnh,sgh->tgns",
                q_local,
                kblk.reshape(tok_rows, groups, HEAD_SIZE),
                preferred_element_type=jnp.float32,
            )
            * scale
        )
        kpos = kstart + jnp.arange(tok_rows, dtype=jnp.int32)
        vis = (
            (kpos[None, :] <= qpos[:, None])
            & (qpos[:, None] - kpos[None, :] < LOOKBACK_WINDOW)
            & (kpos[None, :] >= 0)
            & (doc_ids[:, None] == sblk[None, :])
        )
        vis = vis[:, None, None, :]
        scores = jnp.where(vis, scores, jnp.float32(-1e30))
        newmax = jnp.maximum(rowmax, jnp.max(scores, axis=-1))
        weights = jnp.where(vis, jnp.exp(scores - newmax[..., None]), jnp.float32(0.0))
        factor = jnp.exp(rowmax - newmax)
        total = total * factor + jnp.sum(weights, axis=-1)
        rounded = weights.astype(jnp.bfloat16)
        contrib = jnp.einsum(
            "tgns,sgh->tgnh",
            rounded,
            vblk.reshape(tok_rows, groups, HEAD_SIZE),
            preferred_element_type=jnp.float32,
        )
        accum = accum * factor[..., None] + contrib
        return (newmax, total, accum)

    def attend(state, kblk, vblk, sblk, kstart):
        return work(state, kblk, vblk, sblk, kstart)

    state = (
        jnp.full((tok_rows, groups, QPG), -1e30, jnp.float32),
        jnp.zeros((tok_rows, groups, QPG), jnp.float32),
        jnp.zeros((tok_rows, groups, QPG, HEAD_SIZE), jnp.float32),
    )
    state = attend(state, keys, values, doc_ids, here * tok_rows)

    def chain_step(depth, carry):
        st, kblk, vblk, sblk = carry
        kblk, vblk, sblk = passed_along((kblk, vblk, sblk), "ctx", 1)
        st = attend(st, kblk, vblk, sblk, (here - depth) * tok_rows)
        return (st, kblk, vblk, sblk)

    state = lax.fori_loop(1, reach + 1, chain_step, (state, keys, values, doc_ids))[0]
    rowmax, total, accum = state
    attn = (
        (accum / total[..., None]).astype(jnp.bfloat16).reshape(tok_rows, groups * QPG * HEAD_SIZE)
    )
    partial_sums = jnp.dot(
        attn,
        lax.all_gather(out_weight, "ctx", axis=1, tiled=True),
        preferred_element_type=jnp.float32,
    )
    return lax.psum_scatter(
        partial_sums.astype(jnp.bfloat16), "heads", scatter_dimension=1, tiled=True
    )


def solution(mesh):
    in_specs = (
        P("ctx", "heads"),
        P("ctx", "heads"),
        P("ctx", "heads"),
        P("ctx"),
        P("heads", "ctx"),
    )
    out_specs = P("ctx", "heads")

    def run(queries, keys, values, doc_ids, out_weight):
        n_ctx, n_heads = mesh.shape["ctx"], mesh.shape["heads"]
        local = body
        if fits_fused(n_ctx, n_heads, queries, keys, out_weight):
            local = functools.partial(fused_body, n_ctx, n_heads)
        return jax.shard_map(
            local, mesh=mesh, in_specs=in_specs, out_specs=out_specs, check_vma=False
        )(queries, keys, values, doc_ids, out_weight)

    return run
```

profile of v0, /device:TPU:25, one launch (start us, length us, event | category | flops | bytes accessed | tf_op | source)
XLA Modules:
  0.0 124.7 jit_solution(13938549331121659575)
XLA Ops:
  0.0 0.7 convert_element_type.5
  0.7 1.9 %pad_maximum_fusion.kv_hbm = bf16[272,1024]{1,0:T(8,128)(2,1)} fusion(bf16[16,1024]{1,0:T(8,128)(2,1)S(1)} %broadcast_in_dim.2, bf16[256,512]{1,0:T(8,128)(2,1)} %param.7, bf16[256,512]{1,0:T(8,128)(2,1)} %param.6), kind=kLoop, calls=%fused_computation | loop fusion | flops 1671168 | bytes 1114112 | tf_op jit(solution)/shard_map/concatenate | solution.py:533
  2.6 119.8 %shard_map.55 = bf16[256,2048]{1,0:T(8,128)(2,1)} custom-call(bf16[256,2048]{1,0:T(8,128)(2,1)} %q_ref.1, bf16[272,1024]{1,0:T(8,128)(2,1)} %pad_maximum_fusion.kv_hbm, bf16[2048,256]{1,0:T(8,128)(2,1)} %w_hbm.1), custom_call_target="tpu_custom_call" | custom-call | tf_op jit(solution)/shard_map/pallas_call | solution.py:536
  122.4 2.3 %copy.7 = bf16[256,2048]{1,0:T(8,128)(2,1)} copy(bf16[256,2048]{1,0:T(8,128)(2,1)} %shard_map.55) | data formatting | bytes 2097152
  (2 shorter events, 0.0 us)
where the time goes:
time: 126 us; the launch traced here: 125 us
  Pallas kernels  120 us (95%)
  other arithmetic  2.57 us (2%)
  local copies, waits for them, and re-layouts  2.32 us (2%)
    pallas_call x1, Pallas kernels, fused_body(): pl.pallas_call(functools.partial(fused_kernel, planes, n_heads, groups, t...  120 us

commit v1 on v0

v1 whole, which is shorter than its diff:
```python
import functools
import math

import jax
import jax.numpy as jnp
from jax import lax
from jax.experimental import pallas as pl
from jax.experimental.pallas import tpu as pltpu
from jax.sharding import PartitionSpec as P

HEAD_SIZE = 128
LOOKBACK_WINDOW = 4096
QPG = 4


PLANE = 4
DOC_ROWS = 16
MESH = pl.DeviceIdType.MESH


MASKED = 131072.0


def fused_kernel(
    planes, n_heads, groups, tok, wcols,
    q_ref, docs_ref, k_hbm, v_hbm, w_hbm, out_ref,
    kvbuf, feat, qfeat, wbuf, abuf, acc, rowmax, xsend, xrecv, keep, rsend, obuf,
    local_sem, kv_recv, kvz_send, kvp_send, kvf_send,
    w_recv, w_right, w_left, a_recv, a_send, a_fwd,
    x_send, x_recv, o_send, o_recv,
):
    h = lax.axis_index("heads")
    c = lax.axis_index("ctx")
    z = c // PLANE
    p = c % PLANE
    core = p % 2
    row = p // 2
    mate = p + 1 - 2 * core
    across = (p + 2) % PLANE
    diag = (mate + 2) % PLANE
    last = planes - 1
    per_half = planes // n_heads
    half = wcols // 2
    pair = groups // 2
    part_heads = QPG * pair
    kcols = pair * HEAD_SIZE
    acols = part_heads * HEAD_SIZE
    bf, f32 = jnp.bfloat16, jnp.float32

    def in_plane(other):
        return (h, z * PLANE + other)

    up = (h, c + PLANE)
    down = (h, c - PLANE)

    def copy(src, dst, send, recv, dev):
        return pltpu.make_async_remote_copy(
            src_ref=src, dst_ref=dst, send_sem=send, recv_sem=recv,
            device_id=dev, device_id_type=MESH,
        )

    def kv_up(d, s):
        return copy(
            kvbuf.at[d, p, s], kvbuf.at[d + 1, p, s], kvz_send.at[d, s],
            kv_recv.at[d + 1, p, s], up,
        )

    def kv_side(d, which, s):
        dev = in_plane(mate if which == 0 else across)
        ref = kvbuf.at[d, p, s]
        return copy(ref, ref, kvp_send.at[d, which, s], kv_recv.at[d, p, s], dev)

    def kv_forward(d, s):
        ref = kvbuf.at[d, across, s]
        return copy(ref, ref, kvf_send.at[d, s], kv_recv.at[d, across, s], in_plane(mate))

    def kv_wait(d, who, s):
        ref = kvbuf.at[d, who, s]
        copy(ref, ref, kvf_send.at[d, s], kv_recv.at[d, who, s], in_plane(mate)).wait_recv()

    def w_up(j, s):
        ref = wbuf.at[j, s]
        return copy(ref, ref, w_right.at[j, s], w_recv.at[j, s], up)

    def w_down(j, s):
        ref = wbuf.at[j, s]
        return copy(ref, ref, w_left.at[j, s], w_recv.at[j, s], down)

    def arrive(j, s):
        ref = wbuf.at[j, s]
        copy(ref, ref, w_left.at[j, s], w_recv.at[j, s], in_plane(mate)).wait_recv()

        @pl.when((j > z) & (z > 0))
        def _():
            w_down(j, s).start()

        @pl.when((j < z) & (z < last))
        def _():
            w_up(j, s).start()

    def target(k):
        return jnp.where(k == 0, across, jnp.where(k == 1, diag, jnp.where(k == 2, mate, p)))

    def a_part(who, s):
        return abuf.at[who, s]

    def a_side(which, s):
        dev = in_plane(mate if which == 0 else across)
        return copy(a_part(p, s), a_part(p, s), a_send.at[which, s], a_recv.at[p, s], dev)

    def a_forward(s):
        return copy(
            a_part(across, s), a_part(across, s), a_fwd.at[s], a_recv.at[across, s], in_plane(mate)
        )

    def a_wait(who, s):
        copy(
            a_part(who, s), a_part(who, s), a_fwd.at[s], a_recv.at[who, s], in_plane(mate)
        ).wait_recv()

    def x_copy(u, pp):
        return copy(
            xsend.at[u, pp], xrecv.at[u, pp], x_send.at[u, pp], x_recv.at[u, pp], (1 - h, c)
        )

    def o_copy(u, pp):
        return copy(
            rsend.at[u, pp], obuf.at[u, p], o_send.at[u, pp], o_recv.at[u, p], in_plane(pp)
        )

    kv_in = []
    for s in range(2):
        cols = slice(s * kcols, (s + 1) * kcols)
        mine = kvbuf.at[0, p, s]
        kv_in.append([
            pltpu.make_async_copy(
                k_hbm.at[:, cols], mine.at[0:tok, 0:kcols], local_sem.at[3 * s]
            ),
            pltpu.make_async_copy(
                v_hbm.at[:, cols], mine.at[0:tok, kcols : 2 * kcols], local_sem.at[3 * s + 1]
            ),
            pltpu.make_async_copy(
                docs_ref, mine.at[tok : tok + DOC_ROWS, :], local_sem.at[3 * s + 2]
            ),
        ])
    w_in = [
        pltpu.make_async_copy(
            w_hbm.at[:, s * half : (s + 1) * half], wbuf.at[z, s], local_sem.at[6 + s]
        )
        for s in range(2)
    ]
    for s in range(2):
        for one in kv_in[s]:
            one.start()
    w_in[0].start()
    w_in[1].start()

    barrier = pltpu.get_barrier_semaphore()
    for dev in (in_plane(mate), in_plane(across), in_plane(diag), (1 - h, c)):
        pl.semaphore_signal(barrier, inc=1, device_id=dev, device_id_type=MESH)

    @pl.when(z < last)
    def _():
        pl.semaphore_signal(barrier, inc=1, device_id=up, device_id_type=MESH)

    @pl.when(z > 0)
    def _():
        pl.semaphore_signal(barrier, inc=1, device_id=down, device_id_type=MESH)

    pl.semaphore_wait(barrier, 4 + jnp.minimum(z, 1) + jnp.minimum(last - z, 1))

    for s in range(2):
        for one in kv_in[s]:
            one.wait()

        @pl.when(z < last)
        def _():
            kv_up(0, s).start()

        @pl.when(row == 0)
        def _():
            kv_side(0, 1, s).start()

        @pl.when(core == 0)
        def _():
            kv_side(0, 0, s).start()

    for s in range(2):
        w_in[s].wait()

        @pl.when(z > 0)
        def _():
            w_down(z, s).start()

        @pl.when(z == 0)
        def _():
            w_up(z, s).start()

    factor = HEAD_SIZE ** (-0.5) * math.log2(math.e)

    def same_lane(d, who):
        docs = kvbuf[d, who, 0, tok : tok + DOC_ROWS, 0:tok].astype(f32)[0:1, :]
        column = jnp.broadcast_to(docs, (HEAD_SIZE, tok)).T
        return column == lax.broadcasted_iota(jnp.int32, (tok, HEAD_SIZE), 1).astype(f32)

    def mark(d, lo, count):
        def one(k, carry):
            hit = same_lane(d, lo + k)
            feat[d, lo + k] = jnp.where(hit, jnp.float32(1.0), jnp.float32(0.0)).astype(bf)
            return carry

        lax.fori_loop(0, count, one, 0)

    def attend(d, lo, blocks, s, first):
        ones = jnp.ones((tok, HEAD_SIZE), bf)
        lanes = 2 * HEAD_SIZE
        heads, keys, vals = [], [], []
        for u in range(pair):
            kc = slice(u * HEAD_SIZE, (u + 1) * HEAD_SIZE)
            vc = slice(kcols + u * HEAD_SIZE, kcols + (u + 1) * HEAD_SIZE)
            kb = [
                jnp.concatenate([kvbuf[d, lo + b, s, 0:tok, kc], feat[d, lo + b]], axis=1)
                for b in range(blocks)
            ]
            vb = [
                jnp.concatenate([kvbuf[d, lo + b, s, 0:tok, vc], ones], axis=1)
                for b in range(blocks)
            ]
            for n in range(QPG):
                heads.append(s * part_heads + u * QPG + n)
                keys.append(kb)
                vals.append(vb)
        keys = [jnp.concatenate(kb, axis=0) if blocks > 1 else kb[0] for kb in keys]
        vals = [jnp.concatenate(vb, axis=0) if blocks > 1 else vb[0] for vb in vals]
        if not first:
            olds = [rowmax[head] for head in heads]
            accs = [acc[head] for head in heads]
        done = []
        for n, head in enumerate(heads):
            cols = pl.ds(pl.multiple_of(head * HEAD_SIZE, HEAD_SIZE), HEAD_SIZE)
            qs = jnp.concatenate([q_ref[:, cols], qfeat[...]], axis=1)
            scores = lax.dot_general(
                qs, keys[n], (((1,), (1,)), ((), ())), preferred_element_type=f32
            )
            if first:
                qpos = lax.broadcasted_iota(jnp.int32, (tok, tok), 0)
                kpos = lax.broadcasted_iota(jnp.int32, (tok, tok), 1)
                scores = jnp.where(kpos <= qpos, scores, jnp.float32(-1e30))
            top = functools.reduce(
                jnp.maximum,
                [scores[:, i : i + HEAD_SIZE] for i in range(0, blocks * tok, HEAD_SIZE)],
            )
            top = jnp.max(top, axis=1, keepdims=True)
            if not first:
                top = jnp.maximum(top, olds[n][:, 0:1])
            weights = jnp.exp2((scores - top) * factor).astype(bf)
            both = jnp.dot(weights, vals[n], preferred_element_type=f32)
            if not first:
                shrink = jnp.exp2((olds[n] - top) * factor)
                both = accs[n] * jnp.concatenate([shrink, shrink], axis=1) + both
            done.append((jnp.broadcast_to(top, (tok, HEAD_SIZE)), both))
        for head, (top, both) in zip(heads, done):
            rowmax[head] = top
            acc[head] = both

    def attend_some(d, lo, count, s, most):
        for blocks in range(1, most + 1):

            @pl.when(count == blocks)
            def _():
                attend(d, lo, blocks, s, False)

    qfeat[...] = jnp.where(same_lane(0, p), jnp.float32(0.0), jnp.float32(-MASKED)).astype(bf)
    mark(0, p, 1)

    def own_half(s, carry):
        attend(0, p, 1, s, True)
        return carry

    lax.fori_loop(0, 2, own_half, 0)

    @pl.when(z > 0)
    def _():
        for s in range(2):
            kv_wait(1, p, s)

            @pl.when(z < last)
            def _():
                kv_up(1, s).start()

            kv_side(1, 1, s).start()
            kv_side(1, 0, s).start()

        @pl.when(z < last)
        def _():
            w_up(z, 0).start()
            w_up(z, 1).start()

    def first_plane(s, carry):
        @pl.when(row == 1)
        def _():
            kv_wait(0, across, s)
            kv_forward(0, s).start()

        @pl.when(core == 1)
        def _():
            kv_wait(0, mate, s)

        @pl.when(row == 1)
        def _():
            kv_wait(0, diag, s)

        @pl.when(s == 0)
        def _():
            mark(0, 0, p)

        attend_some(0, 0, p, s, PLANE - 1)
        return carry

    lax.fori_loop(0, 2, first_plane, 0)

    def second_plane(s, carry):
        @pl.when(z < last)
        def _():
            arrive(z + 1, s)

        @pl.when(z > 1)
        def _():
            kv_wait(2, p, s)

            @pl.when(row == 1)
            def _():
                kv_side(2, 1, s).start()

            @pl.when(core == 1)
            def _():
                kv_side(2, 0, s).start()

        @pl.when(z > 0)
        def _():
            kv_wait(1, across, s)
            kv_forward(1, s).start()
            kv_wait(1, mate, s)
            kv_wait(1, diag, s)

            @pl.when(s == 0)
            def _():
                mark(1, 0, PLANE)

            attend(1, 0, PLANE, s, False)

        return carry

    lax.fori_loop(0, 2, second_plane, 0)

    def third_plane(s, carry):
        @pl.when(z > 1)
        def _():
            @pl.when(row == 0)
            def _():
                kv_wait(2, across, s)
                kv_forward(2, s).start()

            @pl.when(core == 0)
            def _():
                kv_wait(2, mate, s)

            @pl.when(row == 0)
            def _():
                kv_wait(2, diag, s)

            @pl.when(s == 0)
            def _():
                mark(2, p, PLANE - p)

            attend_some(2, p, PLANE - p, s, PLANE)

        for n in range(part_heads):
            both = acc[s * part_heads + n]
            attn = both[:, 0:HEAD_SIZE] / both[:, HEAD_SIZE : 2 * HEAD_SIZE]
            abuf[p, s, :, n * HEAD_SIZE : (n + 1) * HEAD_SIZE] = attn.astype(bf)
        a_side(1, s).start()
        a_side(0, s).start()
        return carry

    lax.fori_loop(0, 2, third_plane, 0)

    def order(i):
        if i == 0:
            return z
        if i == 1:
            return jnp.where(z < last, z + 1, z - 1)
        if i == 2:
            return jnp.where(z == 0, 2, jnp.where(z == last, last - 2, z - 1))
        return jnp.where(z < 2, last, 0)

    def place(u, pp, part):
        mine = ((u // 2) // per_half) == h
        uu = u % (2 * per_half)

        @pl.when(mine)
        def _():
            keep[uu, pp] = part

        @pl.when(jnp.logical_not(mine))
        def _():
            xsend[uu, pp] = part.astype(bf)
            x_copy(uu, pp).start()

    def attn_of(pp):
        return jnp.concatenate([abuf[pp, 0], abuf[pp, 1]], axis=1)

    def project(j, lo, hi):
        def rows(k, carry):
            pp = target(k)
            both = jnp.concatenate([wbuf[j, 0], wbuf[j, 1]], axis=1)
            part = jnp.dot(attn_of(pp), both, preferred_element_type=f32)
            place(2 * j, pp, part[:, :half])
            place(2 * j + 1, pp, part[:, half:])
            return carry

        lax.fori_loop(lo, hi, rows, 0)

    def project_half(j, s):
        def rows(k, carry):
            pp = target(k)
            part = jnp.dot(attn_of(pp), wbuf[j, s], preferred_element_type=f32)
            place(2 * j + s, pp, part)
            return carry

        lax.fori_loop(0, PLANE, rows, 0)

    def column(u, src):
        return pl.ds(pl.multiple_of(((u // 2) * PLANE + src) * wcols + (u % 2) * half, half), half)

    def finish(j, s):
        @pl.when((j // per_half) == h)
        def _():
            u = (2 * j + s) % (2 * per_half)

            def rows(k, carry):
                pp = target(k)
                x_copy(u, pp).wait_recv()
                done = (keep[u, pp] + xrecv[u, pp].astype(f32)).astype(bf)

                @pl.when(pp == p)
                def _():
                    out_ref[:, column(u, p)] = done

                @pl.when(pp != p)
                def _():
                    rsend[u, pp] = done
                    o_copy(u, pp).start()

                return carry

            lax.fori_loop(0, PLANE, rows, 0)

    def finish_all(j):
        def one(s, carry):
            finish(j, s)
            return carry

        lax.fori_loop(0, 2, one, 0)

    a_wait(mate, 0)
    a_wait(mate, 1)
    project(order(0), 2, PLANE)

    @pl.when(z == last)
    def _():
        arrive(order(1), 0)
        arrive(order(1), 1)

    project(order(1), 2, PLANE)

    @pl.when(z < last)
    def _():
        arrive(order(2), 0)
        arrive(order(2), 1)
        project(order(2), 2, PLANE)

    @pl.when((z > 0) & (z < last))
    def _():
        arrive(order(3), 0)

    @pl.when(z == 1)
    def _():
        arrive(order(3), 1)

    for s in range(2):
        a_wait(across, s)
        a_forward(s).start()
    for s in range(2):
        a_wait(diag, s)
    project(order(0), 0, 2)
    project(order(1), 0, 2)

    @pl.when(z < last)
    def _():
        project(order(2), 0, 2)

        @pl.when(z == 0)
        def _():
            arrive(order(3), 0)

        @pl.when(z != 1)
        def _():
            arrive(order(3), 1)

        project(order(3), 0, PLANE)
        for i in range(PLANE):
            finish_all(order(i))

    @pl.when(z == last)
    def _():
        arrive(order(2), 0)
        arrive(order(2), 1)
        project(order(2), 0, PLANE)
        finish_all(order(0))
        finish_all(order(1))
        arrive(order(3), 0)
        project_half(order(3), 0)
        finish_all(order(2))
        arrive(order(3), 1)
        project_half(order(3), 1)
        finish_all(order(3))

    def collect(k, carry):
        u = k // PLANE
        src = k % PLANE

        @pl.when(src != p)
        def _():
            copy(
                obuf.at[u, src], obuf.at[u, src], o_send.at[u, src], o_recv.at[u, src],
                in_plane(mate),
            ).wait_recv()
            out_ref[:, column(u, src)] = obuf[u, src]
            o_copy(u, src).wait_send()

        x_copy(u, src).wait_send()
        return carry

    lax.fori_loop(0, 2 * per_half * PLANE, collect, 0)

    for s in range(2):
        a_side(0, s).wait_send()
        a_side(1, s).wait_send()
        a_forward(s).wait_send()

    def w_drain(j, carry):
        @pl.when((j <= z) & (z < last))
        def _():
            w_up(j, 0).wait_send()
            w_up(j, 1).wait_send()

        @pl.when((j >= z) & (z > 0))
        def _():
            w_down(j, 0).wait_send()
            w_down(j, 1).wait_send()

        return carry

    lax.fori_loop(0, planes, w_drain, 0)

    for s in range(2):
        @pl.when(z < last)
        def _():
            kv_up(0, s).wait_send()

            @pl.when(z > 0)
            def _():
                kv_up(1, s).wait_send()

        @pl.when(row == 0)
        def _():
            kv_side(0, 1, s).wait_send()

        @pl.when(core == 0)
        def _():
            kv_side(0, 0, s).wait_send()

        @pl.when(row == 1)
        def _():
            kv_forward(0, s).wait_send()

        @pl.when(z > 0)
        def _():
            kv_side(1, 0, s).wait_send()
            kv_side(1, 1, s).wait_send()
            kv_forward(1, s).wait_send()

        @pl.when(z > 1)
        def _():
            @pl.when(row == 1)
            def _():
                kv_side(2, 1, s).wait_send()

            @pl.when(core == 1)
            def _():
                kv_side(2, 0, s).wait_send()

            @pl.when(row == 0)
            def _():
                kv_forward(2, s).wait_send()


def fused_body(n_ctx, n_heads, queries, keys, values, doc_ids, out_weight):
    tok, qcols = queries.shape
    kdim = keys.shape[1]
    groups = kdim // HEAD_SIZE
    krows, wcols = out_weight.shape
    planes = n_ctx // PLANE
    span = QPG * groups
    per_half = planes // n_heads
    docs = jnp.broadcast_to(
        jnp.pad(doc_ids.astype(jnp.bfloat16), (0, kdim - tok))[None, :], (DOC_ROWS, kdim)
    )
    bf, f32 = jnp.bfloat16, jnp.float32
    dma = pltpu.SemaphoreType.DMA
    anywhere = pl.BlockSpec(memory_space=pl.ANY)
    return pl.pallas_call(
        functools.partial(fused_kernel, planes, n_heads, groups, tok, wcols),
        out_shape=jax.ShapeDtypeStruct((tok, per_half * PLANE * wcols), bf),
        in_specs=[pl.BlockSpec(memory_space=pltpu.VMEM), anywhere, anywhere, anywhere, anywhere],
        out_specs=pl.BlockSpec(memory_space=pltpu.VMEM),
        scratch_shapes=[
            pltpu.VMEM((3, PLANE, 2, tok + DOC_ROWS, kdim), bf),
            pltpu.VMEM((3, PLANE, tok, HEAD_SIZE), bf),
            pltpu.VMEM((tok, HEAD_SIZE), bf),
            pltpu.VMEM((planes, 2, krows, wcols // 2), bf),
            pltpu.VMEM((PLANE, 2, tok, krows // 2), bf),
            pltpu.VMEM((span, tok, 2 * HEAD_SIZE), f32),
            pltpu.VMEM((span, tok, HEAD_SIZE), f32),
            pltpu.VMEM((2 * per_half, PLANE, tok, wcols // 2), bf),
            pltpu.VMEM((2 * per_half, PLANE, tok, wcols // 2), bf),
            pltpu.VMEM((2 * per_half, PLANE, tok, wcols // 2), f32),
            pltpu.VMEM((2 * per_half, PLANE, tok, wcols // 2), bf),
            pltpu.VMEM((2 * per_half, PLANE, tok, wcols // 2), bf),
            dma((8,)),
            dma((3, PLANE, 2)),
            dma((2, 2)),
            dma((3, 2, 2)),
            dma((3, 2)),
            dma((planes, 2)),
            dma((planes, 2)),
            dma((planes, 2)),
            dma((PLANE, 2)),
            dma((2, 2)),
            dma((2,)),
            dma((2 * per_half, PLANE)),
            dma((2 * per_half, PLANE)),
            dma((2 * per_half, PLANE)),
            dma((2 * per_half, PLANE)),
        ],
        compiler_params=pltpu.CompilerParams(
            collective_id=0, has_side_effects=True, vmem_limit_bytes=56 * 1024 * 1024
        ),
    )(queries, docs, keys, values, out_weight)


def fits_fused(n_ctx, n_heads, queries, keys, out_weight):
    tokens = queries.shape[0]
    tok = tokens // n_ctx
    reach = min(LOOKBACK_WINDOW, tokens // 2)
    return (
        n_heads == 2
        and n_ctx % PLANE == 0
        and n_ctx // PLANE == 4
        and tok == 2 * HEAD_SIZE
        and reach == 2 * PLANE * tok
        and reach < LOOKBACK_WINDOW
        and keys.shape[1] // n_heads >= tok
        and (out_weight.shape[1] // n_ctx) % 256 == 0
        and keys.shape[1] // n_heads % (2 * HEAD_SIZE) == 0
    )


def passed_along(block, axis, distance):
    devices = range(lax.axis_size(axis))
    route = [(i - distance, i) for i in devices if i - distance in devices]
    return lax.ppermute(block, axis, route)


def body(queries, keys, values, doc_ids, out_weight):
    tok_rows = queries.shape[0]
    groups = keys.shape[1] // HEAD_SIZE
    scale = HEAD_SIZE ** (-0.5)
    q_local = queries.reshape(tok_rows, groups, QPG, HEAD_SIZE)
    here = lax.axis_index("ctx")
    qpos = here * tok_rows + jnp.arange(tok_rows, dtype=jnp.int32)
    reach = LOOKBACK_WINDOW // tok_rows

    def work(state, kblk, vblk, sblk, kstart):
        rowmax, total, accum = state
        scores = (
            jnp.einsum(
                "tgnh,sgh->tgns",
                q_local,
                kblk.reshape(tok_rows, groups, HEAD_SIZE),
                preferred_element_type=jnp.float32,
            )
            * scale
        )
        kpos = kstart + jnp.arange(tok_rows, dtype=jnp.int32)
        vis = (
            (kpos[None, :] <= qpos[:, None])
            & (qpos[:, None] - kpos[None, :] < LOOKBACK_WINDOW)
            & (kpos[None, :] >= 0)
            & (doc_ids[:, None] == sblk[None, :])
        )
        vis = vis[:, None, None, :]
        scores = jnp.where(vis, scores, jnp.float32(-1e30))
        newmax = jnp.maximum(rowmax, jnp.max(scores, axis=-1))
        weights = jnp.where(vis, jnp.exp(scores - newmax[..., None]), jnp.float32(0.0))
        factor = jnp.exp(rowmax - newmax)
        total = total * factor + jnp.sum(weights, axis=-1)
        rounded = weights.astype(jnp.bfloat16)
        contrib = jnp.einsum(
            "tgns,sgh->tgnh",
            rounded,
            vblk.reshape(tok_rows, groups, HEAD_SIZE),
            preferred_element_type=jnp.float32,
        )
        accum = accum * factor[..., None] + contrib
        return (newmax, total, accum)

    def attend(state, kblk, vblk, sblk, kstart):
        return work(state, kblk, vblk, sblk, kstart)

    state = (
        jnp.full((tok_rows, groups, QPG), -1e30, jnp.float32),
        jnp.zeros((tok_rows, groups, QPG), jnp.float32),
        jnp.zeros((tok_rows, groups, QPG, HEAD_SIZE), jnp.float32),
    )
    state = attend(state, keys, values, doc_ids, here * tok_rows)

    def chain_step(depth, carry):
        st, kblk, vblk, sblk = carry
        kblk, vblk, sblk = passed_along((kblk, vblk, sblk), "ctx", 1)
        st = attend(st, kblk, vblk, sblk, (here - depth) * tok_rows)
        return (st, kblk, vblk, sblk)

    state = lax.fori_loop(1, reach + 1, chain_step, (state, keys, values, doc_ids))[0]
    rowmax, total, accum = state
    attn = (
        (accum / total[..., None]).astype(jnp.bfloat16).reshape(tok_rows, groups * QPG * HEAD_SIZE)
    )
    partial_sums = jnp.dot(
        attn,
        lax.all_gather(out_weight, "ctx", axis=1, tiled=True),
        preferred_element_type=jnp.float32,
    )
    return lax.psum_scatter(
        partial_sums.astype(jnp.bfloat16), "heads", scatter_dimension=1, tiled=True
    )


def solution(mesh):
    in_specs = (
        P("ctx", "heads"),
        P("ctx", "heads"),
        P("ctx", "heads"),
        P("ctx"),
        P("heads", "ctx"),
    )
    out_specs = P("ctx", "heads")

    def run(queries, keys, values, doc_ids, out_weight):
        n_ctx, n_heads = mesh.shape["ctx"], mesh.shape["heads"]
        local = body
        if fits_fused(n_ctx, n_heads, queries, keys, out_weight):
            local = functools.partial(fused_body, n_ctx, n_heads)
        return jax.shard_map(
            local, mesh=mesh, in_specs=in_specs, out_specs=out_specs, check_vma=False
        )(queries, keys, values, doc_ids, out_weight)

    return run
```

time: 126 us -> 111 us (0.88); the launches traced: 125 us -> 111 us
  Pallas kernels: 120 us -> 107 us
  other arithmetic: 2.57 us -> 0.68 us
    pallas_call x1, Pallas kernels: 120 us -> 107 us  [fused_body(): pl.pallas_call(functools.partial(fused_kernel, planes, n_heads, groups, t...]
    concatenate x1 -> x0, other arithmetic: 1.89 us -> none  [fused_body(): jnp.concatenate([jnp.concatenate([keys, values], axis=1), docs], axis=0)]
where the time goes in v1:
time: 111 us
  Pallas kernels  107 us (96%)
  local copies, waits for them, and re-layouts  2.92 us (3%)
    pallas_call x1, Pallas kernels, fused_body(): pl.pallas_call(functools.partial(fused_kernel, planes, n_heads, groups, t...  107 us
    unnamed x1, local copies, waits for them, and re-layouts  2.3 us

profile of v1, /device:TPU:25, one launch (start us, length us, event | category | flops | bytes accessed | tf_op | source)
XLA Modules:
  0.0 111.1 jit_solution(11374285164000579812)
XLA Ops:
  0.0 0.7 convert_element_type.5
  0.7 0.6 broadcast_in_dim.2.docs_ref
  1.3 107.5 %shard_map.55 = bf16[256,2048]{1,0:T(8,128)(2,1)} custom-call(bf16[256,2048]{1,0:T(8,128)(2,1)} %q_ref.1, bf16[16,512]{1,0:T(8,128)(2,1)} %broadcast_in_dim.2.docs_ref, bf16[256,512]{1,0:T(8,128)(2,1)} %k_hbm.1, bf16[256,512]{1,0:T(8,128)(2,1)} %v_hbm.1, bf16[2048,256]{1,0:T(8,128)(2,1)} %w_hbm.1), custom_call_target="tpu_custom_call" | custom-call | tf_op jit(solution)/shard_map/pallas_call | solution.py:623
  108.8 2.3 %copy.7 = bf16[256,2048]{1,0:T(8,128)(2,1)} copy(bf16[256,2048]{1,0:T(8,128)(2,1)} %shard_map.55) | data formatting | bytes 2097152
  (1 shorter events, 0.0 us)

commit v2 on v1

--- a/solution.py
+++ b/solution.py
@@ -24,10 +24,12 @@
 def fused_kernel(
     planes, n_heads, groups, tok, wcols,
     q_ref, docs_ref, k_hbm, v_hbm, w_hbm, out_ref,
-    kvbuf, feat, qfeat, wbuf, abuf, acc, rowmax, xsend, xrecv, keep, rsend, obuf,
+    kvbuf, feat, qfeat, wbuf, abuf, lent, acc, rowmax, xsend, xrecv, keep, rsend, obuf,
+    psend, precv,
     local_sem, kv_recv, kvz_send, kvp_send, kvf_send,
     w_recv, w_right, w_left, a_recv, a_send, a_fwd,
     x_send, x_recv, o_send, o_recv,
+    l_recv, l_down, l_mate, l_across, p_send, p_recv,
 ):
     h = lax.axis_index("heads")
     c = lax.axis_index("ctx")
@@ -39,6 +41,7 @@
     across = (p + 2) % PLANE
     diag = (mate + 2) % PLANE
     last = planes - 1
+    helper = last - 1
     per_half = planes // n_heads
     half = wcols // 2
     pair = groups // 2
@@ -94,7 +97,7 @@
         def _():
             w_down(j, s).start()
 
-        @pl.when((j < z) & (z < last))
+        @pl.when((j < z) & ((z < helper) | ((z == helper) & (j > 0))))
         def _():
             w_up(j, s).start()
 
@@ -117,6 +120,24 @@
         copy(
             a_part(who, s), a_part(who, s), a_fwd.at[s], a_recv.at[who, s], in_plane(mate)
         ).wait_recv()
+
+    def lend_down(who, s, slot):
+        return copy(a_part(who, s), lent.at[who, s], l_down.at[slot], l_recv.at[who, s], down)
+
+    def lend_mate(who, s, slot):
+        ref = lent.at[who, s]
+        return copy(ref, ref, l_mate.at[slot], l_recv.at[who, s], in_plane(mate))
+
+    def lend_across():
+        ref = lent.at[p, 1]
+        return copy(ref, ref, l_across, l_recv.at[p, 1], in_plane(across))
+
+    def lend_wait(who, s):
+        ref = lent.at[who, s]
+        copy(ref, ref, l_mate.at[0], l_recv.at[who, s], in_plane(mate)).wait_recv()
+
+    def give_back(pp):
+        return copy(psend.at[pp], precv.at[pp], p_send.at[pp], p_recv.at[pp], up)
 
     def x_copy(u, pp):
         return copy(
@@ -294,6 +315,9 @@
         @pl.when(z < last)
         def _():
             w_up(z, 0).start()
+
+        @pl.when(z < helper)
+        def _():
             w_up(z, 1).start()
 
     def first_plane(s, carry):
@@ -381,6 +405,15 @@
             abuf[p, s, :, n * HEAD_SIZE : (n + 1) * HEAD_SIZE] = attn.astype(bf)
         a_side(1, s).start()
         a_side(0, s).start()
+
+        @pl.when(z == last)
+        def _():
+            lend_down(p, s, s).start()
+
+        @pl.when((z == helper) & (s == 0))
+        def _():
+            arrive(z - 1, 0)
+
         return carry
 
     lax.fori_loop(0, 2, third_plane, 0)
@@ -389,9 +422,9 @@
         if i == 0:
             return z
         if i == 1:
-            return jnp.where(z < last, z + 1, z - 1)
+            return jnp.where(z < last, z + 1, last - 2)
         if i == 2:
-            return jnp.where(z == 0, 2, jnp.where(z == last, last - 2, z - 1))
+            return jnp.where(z == 0, 2, z - 1)
         return jnp.where(z < 2, last, 0)
 
     def place(u, pp, part):
@@ -430,6 +463,41 @@
 
         lax.fori_loop(0, PLANE, rows, 0)
 
+    def project_lent(lo, hi):
+        def rows(k, carry):
+            pp = target(k)
+            rows_of = jnp.concatenate([lent[pp, 0], lent[pp, 1]], axis=1)
+            both = jnp.concatenate([wbuf[0, 0], wbuf[0, 1]], axis=1)
+            psend[pp] = jnp.dot(rows_of, both, preferred_element_type=f32).astype(bf)
+            give_back(pp).start()
+            return carry
+
+        lax.fori_loop(lo, hi, rows, 0)
+
+    def take_back(lo, hi):
+        def rows(k, carry):
+            pp = target(k)
+            copy(
+                psend.at[pp], precv.at[pp], p_send.at[pp], p_recv.at[pp], in_plane(mate)
+            ).wait_recv()
+            for s in range(2):
+                cols = slice(s * half, (s + 1) * half)
+
+                @pl.when(h == 0)
+                def _():
+                    keep[s, pp] = precv[pp, :, cols].astype(f32)
+
+                @pl.when(h > 0)
+                def _():
+                    copy(
+                        precv.at[pp, :, cols], xrecv.at[s, pp], x_send.at[s, pp],
+                        x_recv.at[s, pp], (1 - h, c),
+                    ).start()
+
+            return carry
+
+        lax.fori_loop(lo, hi, rows, 0)
+
     def column(u, src):
         return pl.ds(pl.multiple_of(((u // 2) * PLANE + src) * wcols + (u % 2) * half, half), half)
 
@@ -467,64 +535,107 @@
     a_wait(mate, 1)
     project(order(0), 2, PLANE)
 
+    @pl.when(z < last)
+    def _():
+        project(order(1), 2, PLANE)
+
+        @pl.when(z < helper)
+        def _():
+            arrive(order(2), 0)
+
+        arrive(order(2), 1)
+
+        @pl.when(z == helper)
+        def _():
+            w_up(z, 1).start()
+
+        project(order(2), 2, PLANE)
+
+    @pl.when(z == 1)
+    def _():
+        arrive(order(3), 0)
+        arrive(order(3), 1)
+
+    @pl.when(z == helper)
+    def _():
+        lend_wait(p, 0)
+        lend_mate(p, 0, 0).start()
+
+    a_wait(across, 0)
+    a_forward(0).start()
+
     @pl.when(z == last)
     def _():
+        lend_down(across, 0, 2).start()
         arrive(order(1), 0)
         arrive(order(1), 1)
 
-    project(order(1), 2, PLANE)
+    a_wait(across, 1)
+    a_forward(1).start()
+
+    @pl.when(z == helper)
+    def _():
+        lend_wait(p, 1)
+        lend_across().start()
+        lend_mate(p, 1, 1).start()
+
+    a_wait(diag, 0)
+    a_wait(diag, 1)
+
+    @pl.when(z == last)
+    def _():
+        project(order(1), 0, PLANE)
+
+    project(order(0), 0, 2)
 
     @pl.when(z < last)
     def _():
-        arrive(order(2), 0)
-        arrive(order(2), 1)
-        project(order(2), 2, PLANE)
-
-    @pl.when((z > 0) & (z < last))
-    def _():
-        arrive(order(3), 0)
-
-    @pl.when(z == 1)
-    def _():
-        arrive(order(3), 1)
-
-    for s in range(2):
-        a_wait(across, s)
-        a_forward(s).start()
-    for s in range(2):
-        a_wait(diag, s)
-    project(order(0), 0, 2)
-    project(order(1), 0, 2)
-
-    @pl.when(z < last)
-    def _():
+        project(order(1), 0, 2)
         project(order(2), 0, 2)
 
-        @pl.when(z == 0)
+        @pl.when(z != 1)
         def _():
             arrive(order(3), 0)
 
+        project_half(order(3), 0)
+
+        @pl.when(z == helper)
+        def _():
+            lend_wait(across, 0)
+            lend_mate(across, 0, 2).start()
+
         @pl.when(z != 1)
         def _():
             arrive(order(3), 1)
 
-        project(order(3), 0, PLANE)
+        @pl.when(z == helper)
+        def _():
+            lend_wait(mate, 0)
+            lend_wait(mate, 1)
+            project_lent(2, PLANE)
+            lend_wait(across, 1)
+            lend_mate(across, 1, 3).start()
+            lend_wait(diag, 0)
+            lend_wait(diag, 1)
+            project_lent(0, 2)
+
+        project_half(order(3), 1)
         for i in range(PLANE):
             finish_all(order(i))
 
     @pl.when(z == last)
     def _():
         arrive(order(2), 0)
+        project_half(order(2), 0)
+        finish_all(order(0))
         arrive(order(2), 1)
-        project(order(2), 0, PLANE)
-        finish_all(order(0))
+        project_half(order(2), 1)
+        take_back(2, PLANE)
+        finish(order(2), 0)
         finish_all(order(1))
-        arrive(order(3), 0)
-        project_half(order(3), 0)
-        finish_all(order(2))
-        arrive(order(3), 1)
-        project_half(order(3), 1)
-        finish_all(order(3))
+        take_back(0, 2)
+        finish(order(2), 1)
+        finish_all(0)
 
     def collect(k, carry):
         u = k // PLANE
@@ -549,8 +660,24 @@
         a_side(1, s).wait_send()
         a_forward(s).wait_send()
 
+    @pl.when(z == last)
+    def _():
+        lend_down(p, 0, 0).wait_send()
+        lend_down(p, 1, 1).wait_send()
+        lend_down(across, 0, 2).wait_send()
+
+    @pl.when(z == helper)
+    def _():
+        lend_across().wait_send()
+        lend_mate(p, 0, 0).wait_send()
+        lend_mate(p, 1, 1).wait_send()
+        lend_mate(across, 0, 2).wait_send()
+        lend_mate(across, 1, 3).wait_send()
+        for pp in range(PLANE):
+            give_back(pp).wait_send()
+
     def w_drain(j, carry):
-        @pl.when((j <= z) & (z < last))
+        @pl.when((j <= z) & ((z < helper) | ((z == helper) & (j > 0))))
         def _():
             w_up(j, 0).wait_send()
             w_up(j, 1).wait_send()
@@ -631,6 +758,7 @@
             pltpu.VMEM((tok, HEAD_SIZE), bf),
             pltpu.VMEM((planes, 2, krows, wcols // 2), bf),
             pltpu.VMEM((PLANE, 2, tok, krows // 2), bf),
+            pltpu.VMEM((PLANE, 2, tok, krows // 2), bf),
             pltpu.VMEM((span, tok, 2 * HEAD_SIZE), f32),
             pltpu.VMEM((span, tok, HEAD_SIZE), f32),
             pltpu.VMEM((2 * per_half, PLANE, tok, wcols // 2), bf),
@@ -638,6 +766,8 @@
             pltpu.VMEM((2 * per_half, PLANE, tok, wcols // 2), f32),
             pltpu.VMEM((2 * per_half, PLANE, tok, wcols // 2), bf),
             pltpu.VMEM((2 * per_half, PLANE, tok, wcols // 2), bf),
+            pltpu.VMEM((PLANE, tok, wcols), bf),
+            pltpu.VMEM((PLANE, tok, wcols), bf),
             dma((8,)),
             dma((3, PLANE, 2)),
             dma((2, 2)),
@@ -653,6 +783,12 @@
             dma((2 * per_half, PLANE)),
             dma((2 * per_half, PLANE)),
             dma((2 * per_half, PLANE)),
+            dma((PLANE, 2)),
+            dma((3,)),
+            dma((4,)),
+            dma,
+            dma((PLANE,)),
+            dma((PLANE,)),
         ],
         compiler_params=pltpu.CompilerParams(
             collective_id=0, has_side_effects=True, vmem_limit_bytes=56 * 1024 * 1024

time: 111 us -> 103 us (0.928)
  Pallas kernels: 107 us -> 98.7 us
    pallas_call x1, Pallas kernels: 107 us -> 98.7 us  [fused_body(): pl.pallas_call(functools.partial(fused_kernel, planes, n_heads, groups, t...]
where the time goes in v2:
time: 103 us; the launch traced here: 102 us
  Pallas kernels  98.7 us (96%)
  local copies, waits for them, and re-layouts  2.92 us (3%)
    pallas_call x1, Pallas kernels, fused_body(): pl.pallas_call(functools.partial(fused_kernel, planes, n_heads, groups, t...  98.7 us
    unnamed x1, local copies, waits for them, and re-layouts  2.3 us

profile of v2, /device:TPU:25, one launch (start us, length us, event | category | flops | bytes accessed | tf_op | source)
XLA Modules:
  0.0 102.4 jit_solution(14856943035960155502)
XLA Ops:
  0.0 0.7 convert_element_type.5
  0.7 0.6 broadcast_in_dim.2.docs_ref
  1.3 98.7 %shard_map.55 = bf16[256,2048]{1,0:T(8,128)(2,1)} custom-call(bf16[256,2048]{1,0:T(8,128)(2,1)} %q_ref.1, bf16[16,512]{1,0:T(8,128)(2,1)} %broadcast_in_dim.2.docs_ref, bf16[256,512]{1,0:T(8,128)(2,1)} %k_hbm.1, bf16[256,512]{1,0:T(8,128)(2,1)} %v_hbm.1, bf16[2048,256]{1,0:T(8,128)(2,1)} %w_hbm.1), custom_call_target="tpu_custom_call" | custom-call | tf_op jit(solution)/shard_map/pallas_call | solution.py:750
  100.1 2.3 %copy.7 = bf16[256,2048]{1,0:T(8,128)(2,1)} copy(bf16[256,2048]{1,0:T(8,128)(2,1)} %shard_map.55) | data formatting | bytes 2097152
  (1 shorter events, 0.0 us)

commit v3 on v2

--- a/solution.py
+++ b/solution.py
@@ -23,13 +23,13 @@
 
 def fused_kernel(
     planes, n_heads, groups, tok, wcols,
-    q_ref, docs_ref, k_hbm, v_hbm, w_hbm, out_ref,
-    kvbuf, feat, qfeat, wbuf, abuf, lent, acc, rowmax, xsend, xrecv, keep, rsend, obuf,
+    q_hbm, docs_hbm, k_hbm, v_hbm, w_hbm, out_ref,
+    q_ref, docs_ref, kvbuf, feat, qfeat, wbuf, abuf, lent, acc, rowmax, xsend, xrecv, keep, rsend,
     psend, precv,
     local_sem, kv_recv, kvz_send, kvp_send, kvf_send,
     w_recv, w_right, w_left, a_recv, a_send, a_fwd,
     x_send, x_recv, o_send, o_recv,
-    l_recv, l_down, l_mate, l_across, p_send, p_recv,
+    l_recv, l_down, l_mate, l_across, p_send, p_recv, o_own,
 ):
     h = lax.axis_index("heads")
     c = lax.axis_index("ctx")
@@ -62,24 +62,30 @@
             device_id=dev, device_id_type=MESH,
         )
 
+    def kv_ref(d, who, s):
+        return kvbuf.at[d, who, 0] if s == 0 else kvbuf.at[d, who, 1, 0:tok]
+
     def kv_up(d, s):
         return copy(
-            kvbuf.at[d, p, s], kvbuf.at[d + 1, p, s], kvz_send.at[d, s],
-            kv_recv.at[d + 1, p, s], up,
+            kv_ref(d, p, s), kv_ref(d + 1, p, s), kvz_send.at[d, s], kv_recv.at[d + 1, p, s], up
         )
 
     def kv_side(d, which, s):
         dev = in_plane(mate if which == 0 else across)
-        ref = kvbuf.at[d, p, s]
+        ref = kv_ref(d, p, s)
         return copy(ref, ref, kvp_send.at[d, which, s], kv_recv.at[d, p, s], dev)
 
     def kv_forward(d, s):
-        ref = kvbuf.at[d, across, s]
+        ref = kv_ref(d, across, s)
         return copy(ref, ref, kvf_send.at[d, s], kv_recv.at[d, across, s], in_plane(mate))
 
     def kv_wait(d, who, s):
-        ref = kvbuf.at[d, who, s]
+        ref = kv_ref(d, who, s)
         copy(ref, ref, kvf_send.at[d, s], kv_recv.at[d, who, s], in_plane(mate)).wait_recv()
+
+    def each(s, act):
+        for v in range(2):
+            pl.when(s == v)(functools.partial(act, v))
 
     def w_up(j, s):
         ref = wbuf.at[j, s]
@@ -144,10 +150,17 @@
             xsend.at[u, pp], xrecv.at[u, pp], x_send.at[u, pp], x_recv.at[u, pp], (1 - h, c)
         )
 
+    def column(u, src):
+        return pl.ds(pl.multiple_of(((u // 2) * PLANE + src) * wcols + (u % 2) * half, half), half)
+
     def o_copy(u, pp):
         return copy(
-            rsend.at[u, pp], obuf.at[u, p], o_send.at[u, pp], o_recv.at[u, p], in_plane(pp)
+            rsend.at[u, pp], out_ref.at[:, column(u, p)], o_send.at[u, pp], o_recv.at[u, p],
+            in_plane(pp),
         )
+
+    def o_local(u):
+        return pltpu.make_async_copy(rsend.at[u, p], out_ref.at[:, column(u, p)], o_own.at[u])
 
     kv_in = []
     for s in range(2):
@@ -160,10 +173,9 @@
             pltpu.make_async_copy(
                 v_hbm.at[:, cols], mine.at[0:tok, kcols : 2 * kcols], local_sem.at[3 * s + 1]
             ),
-            pltpu.make_async_copy(
-                docs_ref, mine.at[tok : tok + DOC_ROWS, :], local_sem.at[3 * s + 2]
-            ),
         ])
+    docs_in = pltpu.make_async_copy(docs_hbm, docs_ref, local_sem.at[2])
+    docs_in.start()
     w_in = [
         pltpu.make_async_copy(
             w_hbm.at[:, s * half : (s + 1) * half], wbuf.at[z, s], local_sem.at[6 + s]
@@ -173,6 +185,8 @@
     for s in range(2):
         for one in kv_in[s]:
             one.start()
+    q_in = pltpu.make_async_copy(q_hbm, q_ref, local_sem.at[8])
+    q_in.start()
     w_in[0].start()
     w_in[1].start()
 
@@ -188,6 +202,10 @@
     def _():
         pl.semaphore_signal(barrier, inc=1, device_id=down, device_id_type=MESH)
 
+    docs_in.wait()
+    kvbuf[0, p, 0, tok : tok + DOC_ROWS, 0:tok] = jnp.broadcast_to(
+        docs_ref[...].astype(f32), (DOC_ROWS, tok)
+    ).astype(bf)
     pl.semaphore_wait(barrier, 4 + jnp.minimum(z, 1) + jnp.minimum(last - z, 1))
 
     for s in range(2):
@@ -298,6 +316,7 @@
         attend(0, p, 1, s, True)
         return carry
 
+    q_in.wait()
     lax.fori_loop(0, 2, own_half, 0)
 
     @pl.when(z > 0)
@@ -321,18 +340,21 @@
             w_up(z, 1).start()
 
     def first_plane(s, carry):
-        @pl.when(row == 1)
-        def _():
-            kv_wait(0, across, s)
-            kv_forward(0, s).start()
-
-        @pl.when(core == 1)
-        def _():
-            kv_wait(0, mate, s)
-
-        @pl.when(row == 1)
-        def _():
-            kv_wait(0, diag, s)
+        def settle(v):
+            @pl.when(row == 1)
+            def _():
+                kv_wait(0, across, v)
+                kv_forward(0, v).start()
+
+            @pl.when(core == 1)
+            def _():
+                kv_wait(0, mate, v)
+
+            @pl.when(row == 1)
+            def _():
+                kv_wait(0, diag, v)
+
+        each(s, settle)
 
         @pl.when(s == 0)
         def _():
@@ -348,24 +370,30 @@
         def _():
             arrive(z + 1, s)
 
+        def pass_on(v):
+            kv_wait(2, p, v)
+
+            @pl.when(row == 1)
+            def _():
+                kv_side(2, 1, v).start()
+
+            @pl.when(core == 1)
+            def _():
+                kv_side(2, 0, v).start()
+
+        def settle(v):
+            kv_wait(1, across, v)
+            kv_forward(1, v).start()
+            kv_wait(1, mate, v)
+            kv_wait(1, diag, v)
+
         @pl.when(z > 1)
         def _():
-            kv_wait(2, p, s)
-
-            @pl.when(row == 1)
-            def _():
-                kv_side(2, 1, s).start()
-
-            @pl.when(core == 1)
-            def _():
-                kv_side(2, 0, s).start()
+            each(s, pass_on)
 
         @pl.when(z > 0)
         def _():
-            kv_wait(1, across, s)
-            kv_forward(1, s).start()
-            kv_wait(1, mate, s)
-            kv_wait(1, diag, s)
+            each(s, settle)
 
             @pl.when(s == 0)
             def _():
@@ -378,20 +406,23 @@
     lax.fori_loop(0, 2, second_plane, 0)
 
     def third_plane(s, carry):
+        def settle(v):
+            @pl.when(row == 0)
+            def _():
+                kv_wait(2, across, v)
+                kv_forward(2, v).start()
+
+            @pl.when(core == 0)
+            def _():
+                kv_wait(2, mate, v)
+
+            @pl.when(row == 0)
+            def _():
+                kv_wait(2, diag, v)
+
         @pl.when(z > 1)
         def _():
-            @pl.when(row == 0)
-            def _():
-                kv_wait(2, across, s)
-                kv_forward(2, s).start()
-
-            @pl.when(core == 0)
-            def _():
-                kv_wait(2, mate, s)
-
-            @pl.when(row == 0)
-            def _():
-                kv_wait(2, diag, s)
+            each(s, settle)
 
             @pl.when(s == 0)
             def _():
@@ -498,31 +529,41 @@
 
         lax.fori_loop(lo, hi, rows, 0)
 
-    def column(u, src):
-        return pl.ds(pl.multiple_of(((u // 2) * PLANE + src) * wcols + (u % 2) * half, half), half)
+    def settle_rows(u, lo, hi):
+        def rows(k, carry):
+            pp = target(k)
+            x_copy(u, pp).wait_recv()
+            rsend[u, pp] = (keep[u, pp] + xrecv[u, pp].astype(f32)).astype(bf)
+
+            @pl.when(pp == p)
+            def _():
+                o_local(u).start()
+
+            @pl.when(pp != p)
+            def _():
+                o_copy(u, pp).start()
+
+            return carry
+
+        lax.fori_loop(lo, hi, rows, 0)
 
     def finish(j, s):
         @pl.when((j // per_half) == h)
         def _():
-            u = (2 * j + s) % (2 * per_half)
-
-            def rows(k, carry):
-                pp = target(k)
-                x_copy(u, pp).wait_recv()
-                done = (keep[u, pp] + xrecv[u, pp].astype(f32)).astype(bf)
-
-                @pl.when(pp == p)
-                def _():
-                    out_ref[:, column(u, p)] = done
-
-                @pl.when(pp != p)
-                def _():
-                    rsend[u, pp] = done
-                    o_copy(u, pp).start()
-
+            settle_rows((2 * j + s) % (2 * per_half), 0, PLANE)
+
+    def finish_rows(lo, hi):
+        @pl.when(h == 0)
+        def _():
+            def one(k, carry):
+                def both(s, inner):
+                    settle_rows(s, k, k + 1)
+                    return inner
+
+                lax.fori_loop(0, 2, both, 0)
                 return carry
 
-            lax.fori_loop(0, PLANE, rows, 0)
+            lax.fori_loop(lo, hi, one, 0)
 
     def finish_all(j):
         def one(s, carry):
@@ -599,6 +640,9 @@
 
         project_half(order(3), 0)
 
+        for i in range(PLANE - 1):
+            finish_all(order(i))
+
         @pl.when(z == helper)
         def _():
             lend_wait(across, 0)
@@ -610,18 +654,17 @@
 
         @pl.when(z == helper)
         def _():
+            lend_wait(across, 1)
+            lend_mate(across, 1, 3).start()
+            project_lent(0, 1)
+            lend_wait(diag, 0)
+            lend_wait(diag, 1)
             lend_wait(mate, 0)
             lend_wait(mate, 1)
-            project_lent(2, PLANE)
-            lend_wait(across, 1)
-            lend_mate(across, 1, 3).start()
-            lend_wait(diag, 0)
-            lend_wait(diag, 1)
-            project_lent(0, 2)
+            project_lent(1, PLANE)
 
         project_half(order(3), 1)
-        for i in range(PLANE):
-            finish_all(order(i))
+        finish_all(order(3))
 
     @pl.when(z == last)
     def _():
@@ -630,12 +673,12 @@
         finish_all(order(0))
         arrive(order(2), 1)
         project_half(order(2), 1)
-        take_back(2, PLANE)
-        finish(order(2), 0)
         finish_all(order(1))
         take_back(0, 2)
-        finish(order(2), 1)
-        finish_all(0)
+        finish_all(order(2))
+        finish_rows(0, 2)
+        take_back(2, PLANE)
+        finish_rows(2, PLANE)
 
     def collect(k, carry):
         u = k // PLANE
@@ -644,11 +687,14 @@
         @pl.when(src != p)
         def _():
             copy(
-                obuf.at[u, src], obuf.at[u, src], o_send.at[u, src], o_recv.at[u, src],
-                in_plane(mate),
+                rsend.at[u, src], out_ref.at[:, column(u, src)], o_send.at[u, src],
+                o_recv.at[u, src], in_plane(mate),
             ).wait_recv()
-            out_ref[:, column(u, src)] = obuf[u, src]
             o_copy(u, src).wait_send()
+
+        @pl.when(src == p)
+        def _():
+            o_local(u).wait()
 
         x_copy(u, src).wait_send()
         return carry
@@ -741,18 +787,18 @@
     planes = n_ctx // PLANE
     span = QPG * groups
     per_half = planes // n_heads
-    docs = jnp.broadcast_to(
-        jnp.pad(doc_ids.astype(jnp.bfloat16), (0, kdim - tok))[None, :], (DOC_ROWS, kdim)
-    )
     bf, f32 = jnp.bfloat16, jnp.float32
     dma = pltpu.SemaphoreType.DMA
+    hbm = functools.partial(pltpu.with_memory_space_constraint, memory_space=pltpu.HBM)
     anywhere = pl.BlockSpec(memory_space=pl.ANY)
     return pl.pallas_call(
         functools.partial(fused_kernel, planes, n_heads, groups, tok, wcols),
         out_shape=jax.ShapeDtypeStruct((tok, per_half * PLANE * wcols), bf),
-        in_specs=[pl.BlockSpec(memory_space=pltpu.VMEM), anywhere, anywhere, anywhere, anywhere],
-        out_specs=pl.BlockSpec(memory_space=pltpu.VMEM),
+        in_specs=[pl.BlockSpec(memory_space=pltpu.HBM)] * 5,
+        out_specs=anywhere,
         scratch_shapes=[
+            pltpu.VMEM((tok, qcols), bf),
+            pltpu.VMEM((1, tok), jnp.int32),
             pltpu.VMEM((3, PLANE, 2, tok + DOC_ROWS, kdim), bf),
             pltpu.VMEM((3, PLANE, tok, HEAD_SIZE), bf),
             pltpu.VMEM((tok, HEAD_SIZE), bf),
@@ -765,10 +811,9 @@
             pltpu.VMEM((2 * per_half, PLANE, tok, wcols // 2), bf),
             pltpu.VMEM((2 * per_half, PLANE, tok, wcols // 2), f32),
             pltpu.VMEM((2 * per_half, PLANE, tok, wcols // 2), bf),
-            pltpu.VMEM((2 * per_half, PLANE, tok, wcols // 2), bf),
             pltpu.VMEM((PLANE, tok, wcols), bf),
             pltpu.VMEM((PLANE, tok, wcols), bf),
-            dma((8,)),
+            dma((9,)),
             dma((3, PLANE, 2)),
             dma((2, 2)),
             dma((3, 2, 2)),
@@ -789,11 +834,12 @@
             dma,
             dma((PLANE,)),
             dma((PLANE,)),
+            dma((2 * per_half,)),
         ],
         compiler_params=pltpu.CompilerParams(
-            collective_id=0, has_side_effects=True, vmem_limit_bytes=56 * 1024 * 1024
+            collective_id=0, has_side_effects=True, vmem_limit_bytes=44 * 1024 * 1024
         ),
-    )(queries, docs, keys, values, out_weight)
+    )(hbm(queries), hbm(doc_ids[None, :]), hbm(keys), hbm(values), hbm(out_weight))
 
 
 def fits_fused(n_ctx, n_heads, queries, keys, out_weight):

time: 103 us -> 97.5 us (0.947)
  Pallas kernels: 98.7 us -> 96.1 us
  local copies, waits for them, and re-layouts: 2.92 us -> 0.97 us
    pallas_call x1, Pallas kernels: 98.7 us -> 96.1 us  [fused_body(): pl.pallas_call(functools.partial(fused_kernel, planes, n_heads, groups, t...]
    unnamed x1, local copies, waits for them, and re-layouts: 2.3 us -> 0.97 us
where the time goes in v3:
time: 97.5 us; the launch traced here: 97.1 us
  Pallas kernels  96.1 us (99%)
    pallas_call x1, Pallas kernels, fused_body(): pl.pallas_call(functools.partial(fused_kernel, planes, n_heads, groups, t...  96.1 us

profile of v3, /device:TPU:25, one launch (start us, length us, event | category | flops | bytes accessed | tf_op | source)
XLA Modules:
  0.0 97.1 jit_solution(664860484845494622)
XLA Ops:
  0.0 96.1 %shard_map.55 = bf16[256,2048]{1,0:T(8,128)(2,1)S(1)} custom-call(bf16[256,2048]{1,0:T(8,128)(2,1)} %q_hbm.1, s32[1,256]{1,0:T(1,128)} %bitcast.1, bf16[256,512]{1,0:T(8,128)(2,1)} %k_hbm.1, bf16[256,512]{1,0:T(8,128)(2,1)} %v_hbm.1, bf16[2048,256]{1,0:T(8,128)(2,1)} %w_hbm.1), custom_call_target="tpu_custom_call" | custom-call | tf_op jit(solution)/shard_map/pallas_call | solution.py:794
  96.1 1.0 %copy.7 = bf16[256,2048]{1,0:T(8,128)(2,1)} copy(bf16[256,2048]{1,0:T(8,128)(2,1)S(1)} %shard_map.55) | data formatting | bytes 2097152

commit v4 on v3

--- a/solution.py
+++ b/solution.py
@@ -640,15 +640,19 @@
 
         project_half(order(3), 0)
 
+        @pl.when(z == helper)
+        def _():
+            arrive(order(3), 1)
+            lend_wait(mate, 0)
+            lend_wait(mate, 1)
+            project_lent(2, PLANE)
+            lend_wait(across, 0)
+            lend_mate(across, 0, 2).start()
+
         for i in range(PLANE - 1):
             finish_all(order(i))
 
-        @pl.when(z == helper)
-        def _():
-            lend_wait(across, 0)
-            lend_mate(across, 0, 2).start()
-
-        @pl.when(z != 1)
+        @pl.when(z == 0)
         def _():
             arrive(order(3), 1)
 
@@ -659,9 +663,7 @@
             project_lent(0, 1)
             lend_wait(diag, 0)
             lend_wait(diag, 1)
-            lend_wait(mate, 0)
-            lend_wait(mate, 1)
-            project_lent(1, PLANE)
+            project_lent(1, 2)
 
         project_half(order(3), 1)
         finish_all(order(3))
@@ -674,11 +676,11 @@
         arrive(order(2), 1)
         project_half(order(2), 1)
         finish_all(order(1))
+        take_back(2, PLANE)
+        finish_all(order(2))
+        finish_rows(2, PLANE)
         take_back(0, 2)
-        finish_all(order(2))
         finish_rows(0, 2)
-        take_back(2, PLANE)
-        finish_rows(2, PLANE)
 
     def collect(k, carry):
         u = k // PLANE

time: 97.5 us -> 98.4 us (level)
  Pallas kernels: 96.1 us -> 97.3 us
    pallas_call x1, Pallas kernels: 96.1 us -> 97.3 us  [fused_body(): pl.pallas_call(functools.partial(fused_kernel, planes, n_heads, groups, t...]
where the time goes in v4:
time: 98.4 us; the launch traced here: 98.3 us
  Pallas kernels  97.3 us (99%)
    pallas_call x1, Pallas kernels, fused_body(): pl.pallas_call(functools.partial(fused_kernel, planes, n_heads, groups, t...  97.3 us

profile of v4, /device:TPU:25, one launch (start us, length us, event | category | flops | bytes accessed | tf_op | source)
XLA Modules:
  0.0 98.3 jit_solution(15789115259567234626)
XLA Ops:
  0.0 97.3 %shard_map.55 = bf16[256,2048]{1,0:T(8,128)(2,1)S(1)} custom-call(bf16[256,2048]{1,0:T(8,128)(2,1)} %q_hbm.1, s32[1,256]{1,0:T(1,128)} %bitcast.1, bf16[256,512]{1,0:T(8,128)(2,1)} %k_hbm.1, bf16[256,512]{1,0:T(8,128)(2,1)} %v_hbm.1, bf16[2048,256]{1,0:T(8,128)(2,1)} %w_hbm.1), custom_call_target="tpu_custom_call" | custom-call | tf_op jit(solution)/shard_map/pallas_call | solution.py:796
  97.3 1.0 copy.7
